TPU v7x, 32 devices: a whole 2x2x4 slice. The times are simulated.
32 devices in a mesh: seq: 8 (over z, core), tp: 4 (over y, x).
Axes of the slice: x: 2, y: 2, z: 4, core: 2. Of those that a mesh axis runs over, the one named last changes fastest.
Arguments:
- q_heads: bfloat16 [1024, 4096], P('seq', 'tp'), may hold values from -200 to 200
- k_heads: bfloat16 [1024, 4096], P('seq', 'tp'), may hold values from -4 to 4
- v_heads: bfloat16 [1024, 4096], P('seq', 'tp'), may hold values from -5 to 5
- grad_attn: bfloat16 [1024, 4096], P('seq', 'tp'), may hold values from -5 to 5
- attn_out: bfloat16 [1024, 4096], P('seq', 'tp'), may hold values from -5 to 5
- gate_q: bfloat16 [1024, 8192], P('seq', 'tp'), may hold values from -5 to 5
- feat_k: bfloat16 [1024, 8192], P('seq', 'tp'), may hold values from -5 to 5
- feat_v: bfloat16 [1024, 8192], P('seq', 'tp'), may hold values from -5 to 5
- conv_out: bfloat16 [1024, 8192], P('seq', 'tp'), may hold values from -5 to 5
- grad_y: bfloat16 [1024, 8192], P('seq', 'tp'), may hold values from -5 to 5
- filters: float32 [64, 128], replicated, may hold values from -0.5 to 0.5
Outputs:
- grad_q: bfloat16 [1024, 4096], P('seq', 'tp')
- grad_k: bfloat16 [1024, 4096], P('seq', 'tp')
- grad_v: bfloat16 [1024, 4096], P('seq', 'tp')
- grad_gate: bfloat16 [1024, 8192], P('seq', 'tp')
- grad_feat_k: bfloat16 [1024, 8192], P('seq', 'tp')
- grad_feat_v: bfloat16 [1024, 8192], P('seq', 'tp')
- grad_filters: float32 [64, 128], replicated
All inputs are finite; a program needn't handle non-finite values.
Results may differ from a plain program's by a relative error of at most 0.014.
Values may be sent and summed in bfloat16 or wider, within the bound.
A program may use at most 64 MiB of HBM per device.

v0:
```python
import jax
import jax.numpy as jnp
from jax import lax
from jax.sharding import PartitionSpec as P

HEADS = 32


def from_behind(value, axis, steps):
    count = lax.axis_size(axis)
    leading, last = (max(0, -steps), min(count, count - steps))
    return lax.ppermute(value, axis, [(source, source + steps) for source in range(leading, last)])


def wire_parts(x):
    high = x.astype(jnp.bfloat16)
    back = lax.optimization_barrier(high).astype(jnp.float32)
    low = (x - back).astype(jnp.bfloat16)
    return (high, low)


def local(
    q_heads,
    k_heads,
    v_heads,
    grad_attn,
    attn_out,
    gate_q,
    feat_k,
    feat_v,
    conv_out,
    grad_y,
    filters,
):
    rows = q_heads.shape[0]
    heads_here = HEADS // lax.axis_size("tp")
    width = q_heads.shape[1] // heads_here
    scale = 1.0 / width**0.5
    shards = lax.axis_size("seq")
    place = lax.axis_index("seq")
    queries = q_heads.reshape(rows, heads_here, width)
    upstream = grad_attn.reshape(rows, heads_here, width)
    keys_here = k_heads.reshape(rows, heads_here, width)
    values_here = v_heads.reshape(rows, heads_here, width)
    delta = jnp.sum(
        upstream.astype(jnp.float32)
        * attn_out.reshape(rows, heads_here, width).astype(jnp.float32),
        axis=2,
    )
    delta_heads = delta.T
    diagonal = jnp.arange(rows)[:, None] >= jnp.arange(rows)[None, :]

    def query_tile(state, key_piece, value_piece, live):
        top, total, acc = state
        count = key_piece.shape[0]
        key_block = key_piece.reshape(count, heads_here, width)
        value_block = value_piece.reshape(count, heads_here, width)
        scores = (
            jnp.einsum("qhd,khd->hqk", queries, key_block, preferred_element_type=jnp.float32)
            * scale
        )
        top_new = jnp.maximum(top, jnp.max(jnp.where(live[None], scores, -1e30), axis=2))
        weights = jnp.where(live[None], jnp.exp(scores - top_new[:, :, None]), 0.0)
        decay = jnp.exp(top - top_new)
        dprob = jnp.einsum(
            "qhd,khd->hqk", upstream, value_block, preferred_element_type=jnp.float32
        )
        term = jnp.einsum(
            "hqk,khd->qhd",
            weights * (dprob - delta_heads[:, :, None]),
            key_block.astype(jnp.float32),
            precision=lax.Precision.HIGHEST,
        )
        return (top_new, total * decay + jnp.sum(weights, axis=2), acc * decay.T[:, :, None] + term)

    zero_rows = jnp.zeros((rows, heads_here, width), jnp.float32)
    state = (
        jnp.full((heads_here, rows), -1e30, jnp.float32),
        jnp.zeros((heads_here, rows), jnp.float32),
        zero_rows,
    )
    state = query_tile(state, k_heads, v_heads, diagonal)

    def relay_keys(back, carry):
        inner, moving = carry
        moving = from_behind((moving[0], moving[1]), "seq", 1)
        valid = place >= back
        live = jnp.broadcast_to(valid, (rows, rows))
        inner = query_tile(inner, moving[0], moving[1], live)
        return (inner, moving)

    state, moved = lax.fori_loop(1, shards, relay_keys, (state, (k_heads, v_heads)))
    top, total, acc = state
    lse = (top + jnp.log(total)).T
    grad_query = acc * (1.0 / total).T[:, :, None] * scale
    lse_high, lse_low = wire_parts(lse)
    delta_high, delta_low = wire_parts(delta)
    stats = jnp.stack([lse_high, lse_low, delta_high, delta_low], axis=1)

    def key_tile(inner, query_piece, upstream_piece, stat_piece, live):
        key_grad, value_grad = inner
        count = query_piece.shape[0]
        query_block = query_piece.reshape(count, heads_here, width)
        upstream_block = upstream_piece.reshape(count, heads_here, width)
        lse_w = stat_piece[:, 0].astype(jnp.float32) + stat_piece[:, 1].astype(jnp.float32)
        delta_w = stat_piece[:, 2].astype(jnp.float32) + stat_piece[:, 3].astype(jnp.float32)
        scores = (
            jnp.einsum("qhd,khd->hqk", query_block, keys_here, preferred_element_type=jnp.float32)
            * scale
        )
        probs = jnp.where(live[None], jnp.exp(scores - lse_w.T[:, :, None]), 0.0)
        dprob = jnp.einsum(
            "qhd,khd->hqk", upstream_block, values_here, preferred_element_type=jnp.float32
        )
        dscore = probs * (dprob - delta_w.T[:, :, None])
        value_grad = value_grad + jnp.einsum(
            "hqk,qhd->khd",
            probs.astype(jnp.bfloat16),
            upstream_block,
            preferred_element_type=jnp.float32,
        )
        key_grad = key_grad + jnp.einsum(
            "hqk,qhd->khd",
            dscore.astype(jnp.bfloat16),
            query_block,
            preferred_element_type=jnp.float32,
        )
        return (key_grad, value_grad)

    grads = (zero_rows, zero_rows)
    grads = key_tile(grads, q_heads, grad_attn, stats, diagonal)

    def relay_queries(back, carry):
        inner, moving = carry
        moving = from_behind((moving[0], moving[1], moving[2]), "seq", -1)
        valid = place + back <= shards - 1
        live = jnp.broadcast_to(valid, (rows, rows))
        inner = key_tile(inner, moving[0], moving[1], moving[2], live)
        return (inner, moving)

    grads, moved = lax.fori_loop(1, shards, relay_queries, (grads, (q_heads, grad_attn, stats)))
    key_grad, value_grad = grads
    grad_q = grad_query.astype(jnp.bfloat16).reshape(rows, heads_here * width)
    grad_k = (key_grad * scale).astype(jnp.bfloat16).reshape(rows, heads_here * width)
    grad_v = value_grad.astype(jnp.bfloat16).reshape(rows, heads_here * width)
    span_taps = filters.shape[1]
    groups = filters.shape[0]
    channels = gate_q.shape[1]
    dz = (grad_y.astype(jnp.float32) * gate_q.astype(jnp.float32)).astype(jnp.bfloat16)
    rim = from_behind(dz[: span_taps - 1], "seq", -1)
    grad_gate = (grad_y.astype(jnp.float32) * conv_out.astype(jnp.float32)).astype(jnp.bfloat16)
    padded = jnp.concatenate([dz, rim], axis=0).astype(jnp.float32)
    taps = jnp.tile(filters.T, (1, channels // groups))
    mixed = feat_k.astype(jnp.float32) * feat_v.astype(jnp.float32)
    numbers = ("NWC", "WIO", "NWC")
    dw = lax.conv_general_dilated(
        padded[None],
        taps[:, None, :],
        (1,),
        "VALID",
        dimension_numbers=numbers,
        feature_group_count=channels,
        precision=lax.Precision.HIGHEST,
    )[0]
    local_terms = lax.conv_general_dilated(
        padded[None],
        mixed[:, None, :],
        (1,),
        "VALID",
        dimension_numbers=numbers,
        feature_group_count=channels,
        precision=lax.Precision.HIGHEST,
    )[0]
    grad_feat_k = (dw * feat_v.astype(jnp.float32)).astype(jnp.bfloat16)
    grad_feat_v = (dw * feat_k.astype(jnp.float32)).astype(jnp.bfloat16)
    local_terms = jnp.sum(local_terms.reshape(span_taps, channels // groups, groups), axis=1).T
    filter_total = lax.psum(local_terms, ("seq", "tp"))
    count_all = rows * shards * channels * lax.axis_size("tp") / groups
    grad_filters = filter_total * (1.0 / count_all**0.5)
    return (grad_q, grad_k, grad_v, grad_gate, grad_feat_k, grad_feat_v, grad_filters)


def solution(mesh):
    in_specs = (
        P("seq", "tp"),
        P("seq", "tp"),
        P("seq", "tp"),
        P("seq", "tp"),
        P("seq", "tp"),
        P("seq", "tp"),
        P("seq", "tp"),
        P("seq", "tp"),
        P("seq", "tp"),
        P("seq", "tp"),
        P(),
    )
    out_specs = (
        P("seq", "tp"),
        P("seq", "tp"),
        P("seq", "tp"),
        P("seq", "tp"),
        P("seq", "tp"),
        P("seq", "tp"),
        P(),
    )
    return jax.shard_map(local, mesh=mesh, in_specs=in_specs, out_specs=out_specs, check_vma=False)
```

profile of v0, /device:TPU:0, one launch (start us, length us, event | category | flops | bytes accessed | tf_op | source)
XLA Modules:
  0.0 252.8 jit_solution(9573498819342594499)
XLA Ops:
  8.7 79.7 %while.42 = (s32[]{:T(128)}, f32[8,128]{1,0:T(8,128)S(1)}, f32[8,128]{1,0:T(8,128)S(1)}, f32[128,8,128]{2,0,1:T(8,128)S(1)}, bf16[128,1024]{0,1:T(8,128)(2,1)S(1...) while((s32[]{:T(128)}, f32[8,128]{1,0:T(8,128)S(1)}, ...), condition=%wide.region_6.7_spmd, body=%wide.region_3.6_spmd.sunk | while | flops 270011392 | bytes 8196297 | solution.py:92
  11.7 4.6 %collective-permute-start.1 = (bf16[128,1024]{0,1:T(8,128)(2,1)S(1)}, bf16[128,1024]{0,1:T(8,128)(2,1)S(1)}, u32[]{:S(2)}, u32[]{:S(2)}) collective-permute-start(bf16[128,1024]{0,1:T(8,128)(2,1)S(1)} %get-tuple-element.619), channel_id=1, source_target_pairs={{0,4},{4,8},{8,12},{12,16},{16,20},{20,24},{24,28},{1,5},{5,9},{9,... | collective-permute-start | bytes 786440 | tf_op jit(solution)/shard_map/while/body/eval_jaxpr/ppermute | solution.py:12
  18.6 5.0 %collective-permute-start = (bf16[128,1024]{0,1:T(8,128)(2,1)S(1)}, bf16[128,1024]{0,1:T(8,128)(2,1)S(1)}, u32[]{:S(2)}, u32[]{:S(2)}) collective-permute-start(bf16[128,1024]{0,1:T(8,128)(2,1)S(1)} %get-tuple-element.618), channel_id=1, source_target_pairs={{0,4},{4,8},{8,12},{12,16},{16,20},{20,24},{24,28},{1,5},{5,9},{9,... | collective-permute-start | bytes 786440 | tf_op jit(solution)/shard_map/while/body/eval_jaxpr/ppermute | solution.py:12
  23.5 4.4 %collective-permute-start.1 = (bf16[128,1024]{0,1:T(8,128)(2,1)S(1)}, bf16[128,1024]{0,1:T(8,128)(2,1)S(1)}, u32[]{:S(2)}, u32[]{:S(2)}) collective-permute-start(bf16[128,1024]{0,1:T(8,128)(2,1)S(1)} %get-tuple-element.619), channel_id=1, source_target_pairs={{0,4},{4,8},{8,12},{12,16},{16,20},{20,24},{24,28},{1,5},{5,9},{9,... | collective-permute-start | bytes 786440 | tf_op jit(solution)/shard_map/while/body/eval_jaxpr/ppermute | solution.py:12
  30.2 5.0 %collective-permute-start = (bf16[128,1024]{0,1:T(8,128)(2,1)S(1)}, bf16[128,1024]{0,1:T(8,128)(2,1)S(1)}, u32[]{:S(2)}, u32[]{:S(2)}) collective-permute-start(bf16[128,1024]{0,1:T(8,128)(2,1)S(1)} %get-tuple-element.618), channel_id=1, source_target_pairs={{0,4},{4,8},{8,12},{12,16},{16,20},{20,24},{24,28},{1,5},{5,9},{9,... | collective-permute-start | bytes 786440 | tf_op jit(solution)/shard_map/while/body/eval_jaxpr/ppermute | solution.py:12
  35.2 4.4 %collective-permute-start.1 = (bf16[128,1024]{0,1:T(8,128)(2,1)S(1)}, bf16[128,1024]{0,1:T(8,128)(2,1)S(1)}, u32[]{:S(2)}, u32[]{:S(2)}) collective-permute-start(bf16[128,1024]{0,1:T(8,128)(2,1)S(1)} %get-tuple-element.619), channel_id=1, source_target_pairs={{0,4},{4,8},{8,12},{12,16},{16,20},{20,24},{24,28},{1,5},{5,9},{9,... | collective-permute-start | bytes 786440 | tf_op jit(solution)/shard_map/while/body/eval_jaxpr/ppermute | solution.py:12
  41.8 5.0 %collective-permute-start = (bf16[128,1024]{0,1:T(8,128)(2,1)S(1)}, bf16[128,1024]{0,1:T(8,128)(2,1)S(1)}, u32[]{:S(2)}, u32[]{:S(2)}) collective-permute-start(bf16[128,1024]{0,1:T(8,128)(2,1)S(1)} %get-tuple-element.618), channel_id=1, source_target_pairs={{0,4},{4,8},{8,12},{12,16},{16,20},{20,24},{24,28},{1,5},{5,9},{9,... | collective-permute-start | bytes 786440 | tf_op jit(solution)/shard_map/while/body/eval_jaxpr/ppermute | solution.py:12
  46.8 4.4 %collective-permute-start.1 = (bf16[128,1024]{0,1:T(8,128)(2,1)S(1)}, bf16[128,1024]{0,1:T(8,128)(2,1)S(1)}, u32[]{:S(2)}, u32[]{:S(2)}) collective-permute-start(bf16[128,1024]{0,1:T(8,128)(2,1)S(1)} %get-tuple-element.619), channel_id=1, source_target_pairs={{0,4},{4,8},{8,12},{12,16},{16,20},{20,24},{24,28},{1,5},{5,9},{9,... | collective-permute-start | bytes 786440 | tf_op jit(solution)/shard_map/while/body/eval_jaxpr/ppermute | solution.py:12
  53.5 5.0 %collective-permute-start = (bf16[128,1024]{0,1:T(8,128)(2,1)S(1)}, bf16[128,1024]{0,1:T(8,128)(2,1)S(1)}, u32[]{:S(2)}, u32[]{:S(2)}) collective-permute-start(bf16[128,1024]{0,1:T(8,128)(2,1)S(1)} %get-tuple-element.618), channel_id=1, source_target_pairs={{0,4},{4,8},{8,12},{12,16},{16,20},{20,24},{24,28},{1,5},{5,9},{9,... | collective-permute-start | bytes 786440 | tf_op jit(solution)/shard_map/while/body/eval_jaxpr/ppermute | solution.py:12
  58.4 4.4 %collective-permute-start.1 = (bf16[128,1024]{0,1:T(8,128)(2,1)S(1)}, bf16[128,1024]{0,1:T(8,128)(2,1)S(1)}, u32[]{:S(2)}, u32[]{:S(2)}) collective-permute-start(bf16[128,1024]{0,1:T(8,128)(2,1)S(1)} %get-tuple-element.619), channel_id=1, source_target_pairs={{0,4},{4,8},{8,12},{12,16},{16,20},{20,24},{24,28},{1,5},{5,9},{9,... | collective-permute-start | bytes 786440 | tf_op jit(solution)/shard_map/while/body/eval_jaxpr/ppermute | solution.py:12
  65.1 5.0 %collective-permute-start = (bf16[128,1024]{0,1:T(8,128)(2,1)S(1)}, bf16[128,1024]{0,1:T(8,128)(2,1)S(1)}, u32[]{:S(2)}, u32[]{:S(2)}) collective-permute-start(bf16[128,1024]{0,1:T(8,128)(2,1)S(1)} %get-tuple-element.618), channel_id=1, source_target_pairs={{0,4},{4,8},{8,12},{12,16},{16,20},{20,24},{24,28},{1,5},{5,9},{9,... | collective-permute-start | bytes 786440 | tf_op jit(solution)/shard_map/while/body/eval_jaxpr/ppermute | solution.py:12
  70.1 4.4 %collective-permute-start.1 = (bf16[128,1024]{0,1:T(8,128)(2,1)S(1)}, bf16[128,1024]{0,1:T(8,128)(2,1)S(1)}, u32[]{:S(2)}, u32[]{:S(2)}) collective-permute-start(bf16[128,1024]{0,1:T(8,128)(2,1)S(1)} %get-tuple-element.619), channel_id=1, source_target_pairs={{0,4},{4,8},{8,12},{12,16},{16,20},{20,24},{24,28},{1,5},{5,9},{9,... | collective-permute-start | bytes 786440 | tf_op jit(solution)/shard_map/while/body/eval_jaxpr/ppermute | solution.py:12
  76.7 5.0 %collective-permute-start = (bf16[128,1024]{0,1:T(8,128)(2,1)S(1)}, bf16[128,1024]{0,1:T(8,128)(2,1)S(1)}, u32[]{:S(2)}, u32[]{:S(2)}) collective-permute-start(bf16[128,1024]{0,1:T(8,128)(2,1)S(1)} %get-tuple-element.618), channel_id=1, source_target_pairs={{0,4},{4,8},{8,12},{12,16},{16,20},{20,24},{24,28},{1,5},{5,9},{9,... | collective-permute-start | bytes 786440 | tf_op jit(solution)/shard_map/while/body/eval_jaxpr/ppermute | solution.py:12
  81.7 4.4 %collective-permute-start.1 = (bf16[128,1024]{0,1:T(8,128)(2,1)S(1)}, bf16[128,1024]{0,1:T(8,128)(2,1)S(1)}, u32[]{:S(2)}, u32[]{:S(2)}) collective-permute-start(bf16[128,1024]{0,1:T(8,128)(2,1)S(1)} %get-tuple-element.619), channel_id=1, source_target_pairs={{0,4},{4,8},{8,12},{12,16},{16,20},{20,24},{24,28},{1,5},{5,9},{9,... | collective-permute-start | bytes 786440 | tf_op jit(solution)/shard_map/while/body/eval_jaxpr/ppermute | solution.py:12
  89.8 87.0 %while.43 = (s32[]{:T(128)}, f32[128,8,128]{2,0,1:T(8,128)S(1)}, f32[128,8,128]{2,0,1:T(8,128)S(1)}, bf16[128,1024]{0,1:T(8,128)(2,1)S(1)}, bf16[128,1024]{0,1:T...) while((s32[]{:T(128)}, f32[128,8,128]{2,0,1:T(8,128)S(1)}, ...), condition=%wide.region_8.9_spmd, body=%wide.region_7.8_spmd.sunk | while | flops 135403520 | bytes 8462587 | solution.py:141
  104.5 6.1 %collective-permute-done.3 = bf16[128,4,8]{0,2,1:T(8,128)(2,1)S(1)} collective-permute-done((bf16[128,4,8]{0,2,1:T(8,128)(2,1)S(1)}, bf16[128,4,8]{0,2,1:T(8,128)(2,1)S(1)}, u32[]{:S(2)}, u32[]{:S(2)}) %collective-permute-start.3) | collective-permute-done | bytes 8224 | tf_op jit(solution)/shard_map/while/body/eval_jaxpr/ppermute | solution.py:12
  117.8 5.4 %collective-permute-done.3 = bf16[128,4,8]{0,2,1:T(8,128)(2,1)S(1)} collective-permute-done((bf16[128,4,8]{0,2,1:T(8,128)(2,1)S(1)}, bf16[128,4,8]{0,2,1:T(8,128)(2,1)S(1)}, u32[]{:S(2)}, u32[]{:S(2)}) %collective-permute-start.3) | collective-permute-done | bytes 8224 | tf_op jit(solution)/shard_map/while/body/eval_jaxpr/ppermute | solution.py:12
  130.4 5.4 %collective-permute-done.3 = bf16[128,4,8]{0,2,1:T(8,128)(2,1)S(1)} collective-permute-done((bf16[128,4,8]{0,2,1:T(8,128)(2,1)S(1)}, bf16[128,4,8]{0,2,1:T(8,128)(2,1)S(1)}, u32[]{:S(2)}, u32[]{:S(2)}) %collective-permute-start.3) | collective-permute-done | bytes 8224 | tf_op jit(solution)/shard_map/while/body/eval_jaxpr/ppermute | solution.py:12
  143.0 5.3 %collective-permute-done.3 = bf16[128,4,8]{0,2,1:T(8,128)(2,1)S(1)} collective-permute-done((bf16[128,4,8]{0,2,1:T(8,128)(2,1)S(1)}, bf16[128,4,8]{0,2,1:T(8,128)(2,1)S(1)}, u32[]{:S(2)}, u32[]{:S(2)}) %collective-permute-start.3) | collective-permute-done | bytes 8224 | tf_op jit(solution)/shard_map/while/body/eval_jaxpr/ppermute | solution.py:12
  155.5 5.3 %collective-permute-done.3 = bf16[128,4,8]{0,2,1:T(8,128)(2,1)S(1)} collective-permute-done((bf16[128,4,8]{0,2,1:T(8,128)(2,1)S(1)}, bf16[128,4,8]{0,2,1:T(8,128)(2,1)S(1)}, u32[]{:S(2)}, u32[]{:S(2)}) %collective-permute-start.3) | collective-permute-done | bytes 8224 | tf_op jit(solution)/shard_map/while/body/eval_jaxpr/ppermute | solution.py:12
  168.1 5.3 %collective-permute-done.3 = bf16[128,4,8]{0,2,1:T(8,128)(2,1)S(1)} collective-permute-done((bf16[128,4,8]{0,2,1:T(8,128)(2,1)S(1)}, bf16[128,4,8]{0,2,1:T(8,128)(2,1)S(1)}, u32[]{:S(2)}, u32[]{:S(2)}) %collective-permute-start.3) | collective-permute-done | bytes 8224 | tf_op jit(solution)/shard_map/while/body/eval_jaxpr/ppermute | solution.py:12
  181.6 11.6 %fusion.15 = f32[1,128,2048]{2,0,1:T(1,128)S(1)} fusion(f32[128,1,2048]{2,1,0:T(1,128)S(1)} %copy.197, bf16[1,255,2048]{2,1,0:T(8,128)(2,1)S(1)} %maximum_bitcast_fusion), kind=kOutput, calls=%fused_computation.28 | convolution fusion | flops 402653184 | bytes 3141632 | tf_op jit(solution)/shard_map/conv_general_dilated | solution.py:156
  194.7 11.7 %fusion.13 = f32[1,128,2048]{2,0,1:T(1,128)S(1)} fusion(bf16[1,255,2048]{2,1,0:T(8,128)(2,1)S(1)} %maximum_bitcast_fusion, f32[128,1,2048]{2,0,1:T(8,128)S(1)} %get-tuple-element.462), kind=kOutput, calls=%fused_computation.26 | convolution fusion | flops 402653184 | bytes 3141632 | tf_op jit(solution)/shard_map/conv_general_dilated | solution.py:165
  207.2 44.9 %psum.7 = f32[64,128]{1,0:T(8,128)S(1)} all-reduce(f32[64,128]{1,0:T(8,128)S(1)} %bitcast.177), channel_id=1, replica_groups=mesh['seq'=8,'tp'=4] {'seq','tp'}, use_global_device_ids=true, to_apply=%region_10.11 | all-reduce | flops 8192 | bytes 65536 | tf_op jit(solution)/shard_map/psum | solution.py:177
  (230 shorter events, 88.8 us)
Async XLA Ops:
  3.4 176.9 %collective-permute-start.5 = (bf16[127,2048]{1,0:T(8,128)(2,1)}, bf16[127,2048]{1,0:T(8,128)(2,1)}, u32[]{:S(2)}, u32[]{:S(2)}) collective-permute-start(bf16[127,2048]{1,0:T(8,128)(2,1)} %bitcast.110), channel_id=1, source_target_pairs={{4,0},{8,4},{12,8},{16,12},{20,16},{24,20},{28,24},{5,1},{9,5},{13... | collective-permute-start | bytes 1560584 | tf_op jit(solution)/shard_map/ppermute | solution.py:12
  18.6 9.4 %collective-permute-start = (bf16[128,1024]{0,1:T(8,128)(2,1)S(1)}, bf16[128,1024]{0,1:T(8,128)(2,1)S(1)}, u32[]{:S(2)}, u32[]{:S(2)}) collective-permute-start(bf16[128,1024]{0,1:T(8,128)(2,1)S(1)} %get-tuple-element.618), channel_id=1, source_target_pairs={{0,4},{4,8},{8,12},{12,16},{16,20},{20,24},{24,28},{1,5},{5,9},{9,... | collective-permute-start | bytes 786440 | tf_op jit(solution)/shard_map/while/body/eval_jaxpr/ppermute | solution.py:12
  30.2 9.4 %collective-permute-start = (bf16[128,1024]{0,1:T(8,128)(2,1)S(1)}, bf16[128,1024]{0,1:T(8,128)(2,1)S(1)}, u32[]{:S(2)}, u32[]{:S(2)}) collective-permute-start(bf16[128,1024]{0,1:T(8,128)(2,1)S(1)} %get-tuple-element.618), channel_id=1, source_target_pairs={{0,4},{4,8},{8,12},{12,16},{16,20},{20,24},{24,28},{1,5},{5,9},{9,... | collective-permute-start | bytes 786440 | tf_op jit(solution)/shard_map/while/body/eval_jaxpr/ppermute | solution.py:12
  41.8 9.4 %collective-permute-start = (bf16[128,1024]{0,1:T(8,128)(2,1)S(1)}, bf16[128,1024]{0,1:T(8,128)(2,1)S(1)}, u32[]{:S(2)}, u32[]{:S(2)}) collective-permute-start(bf16[128,1024]{0,1:T(8,128)(2,1)S(1)} %get-tuple-element.618), channel_id=1, source_target_pairs={{0,4},{4,8},{8,12},{12,16},{16,20},{20,24},{24,28},{1,5},{5,9},{9,... | collective-permute-start | bytes 786440 | tf_op jit(solution)/shard_map/while/body/eval_jaxpr/ppermute | solution.py:12
  53.5 9.4 %collective-permute-start = (bf16[128,1024]{0,1:T(8,128)(2,1)S(1)}, bf16[128,1024]{0,1:T(8,128)(2,1)S(1)}, u32[]{:S(2)}, u32[]{:S(2)}) collective-permute-start(bf16[128,1024]{0,1:T(8,128)(2,1)S(1)} %get-tuple-element.618), channel_id=1, source_target_pairs={{0,4},{4,8},{8,12},{12,16},{16,20},{20,24},{24,28},{1,5},{5,9},{9,... | collective-permute-start | bytes 786440 | tf_op jit(solution)/shard_map/while/body/eval_jaxpr/ppermute | solution.py:12
  65.1 9.4 %collective-permute-start = (bf16[128,1024]{0,1:T(8,128)(2,1)S(1)}, bf16[128,1024]{0,1:T(8,128)(2,1)S(1)}, u32[]{:S(2)}, u32[]{:S(2)}) collective-permute-start(bf16[128,1024]{0,1:T(8,128)(2,1)S(1)} %get-tuple-element.618), channel_id=1, source_target_pairs={{0,4},{4,8},{8,12},{12,16},{16,20},{20,24},{24,28},{1,5},{5,9},{9,... | collective-permute-start | bytes 786440 | tf_op jit(solution)/shard_map/while/body/eval_jaxpr/ppermute | solution.py:12
  76.7 9.4 %collective-permute-start = (bf16[128,1024]{0,1:T(8,128)(2,1)S(1)}, bf16[128,1024]{0,1:T(8,128)(2,1)S(1)}, u32[]{:S(2)}, u32[]{:S(2)}) collective-permute-start(bf16[128,1024]{0,1:T(8,128)(2,1)S(1)} %get-tuple-element.618), channel_id=1, source_target_pairs={{0,4},{4,8},{8,12},{12,16},{16,20},{20,24},{24,28},{1,5},{5,9},{9,... | collective-permute-start | bytes 786440 | tf_op jit(solution)/shard_map/while/body/eval_jaxpr/ppermute | solution.py:12
  100.6 10.0 %collective-permute-start.2 = (bf16[128,1024]{0,1:T(8,128)(2,1)S(1)}, bf16[128,1024]{0,1:T(8,128)(2,1)S(1)}, u32[]{:S(2)}, u32[]{:S(2)}) collective-permute-start(bf16[128,1024]{0,1:T(8,128)(2,1)S(1)} %get-tuple-element.650), channel_id=1, source_target_pairs={{4,0},{8,4},{12,8},{16,12},{20,16},{24,20},{28,24},{5,1},{9,5},{13... | collective-permute-start | bytes 786440 | tf_op jit(solution)/shard_map/while/body/eval_jaxpr/ppermute | solution.py:12
  101.9 8.7 %collective-permute-start.3 = (bf16[128,4,8]{0,2,1:T(8,128)(2,1)S(1)}, bf16[128,4,8]{0,2,1:T(8,128)(2,1)S(1)}, u32[]{:S(2)}, u32[]{:S(2)}) collective-permute-start(bf16[128,4,8]{0,2,1:T(8,128)(2,1)S(1)} %get-tuple-element.652), channel_id=1, source_target_pairs={{4,0},{8,4},{12,8},{16,12},{20,16},{24,20},{28,24},{5,1},{9,5},{13... | collective-permute-start | bytes 24584 | tf_op jit(solution)/shard_map/while/body/eval_jaxpr/ppermute | solution.py:12
  103.2 9.7 %collective-permute-start.4 = (bf16[128,1024]{0,1:T(8,128)(2,1)S(1)}, bf16[128,1024]{0,1:T(8,128)(2,1)S(1)}, u32[]{:S(2)}, u32[]{:S(2)}) collective-permute-start(bf16[128,1024]{0,1:T(8,128)(2,1)S(1)} %get-tuple-element.651), channel_id=1, source_target_pairs={{4,0},{8,4},{12,8},{16,12},{20,16},{24,20},{28,24},{5,1},{9,5},{13... | collective-permute-start | bytes 786440 | tf_op jit(solution)/shard_map/while/body/eval_jaxpr/ppermute | solution.py:12
  113.9 9.3 %collective-permute-start.2 = (bf16[128,1024]{0,1:T(8,128)(2,1)S(1)}, bf16[128,1024]{0,1:T(8,128)(2,1)S(1)}, u32[]{:S(2)}, u32[]{:S(2)}) collective-permute-start(bf16[128,1024]{0,1:T(8,128)(2,1)S(1)} %get-tuple-element.650), channel_id=1, source_target_pairs={{4,0},{8,4},{12,8},{16,12},{20,16},{24,20},{28,24},{5,1},{9,5},{13... | collective-permute-start | bytes 786440 | tf_op jit(solution)/shard_map/while/body/eval_jaxpr/ppermute | solution.py:12
  115.2 8.0 %collective-permute-start.3 = (bf16[128,4,8]{0,2,1:T(8,128)(2,1)S(1)}, bf16[128,4,8]{0,2,1:T(8,128)(2,1)S(1)}, u32[]{:S(2)}, u32[]{:S(2)}) collective-permute-start(bf16[128,4,8]{0,2,1:T(8,128)(2,1)S(1)} %get-tuple-element.652), channel_id=1, source_target_pairs={{4,0},{8,4},{12,8},{16,12},{20,16},{24,20},{28,24},{5,1},{9,5},{13... | collective-permute-start | bytes 24584 | tf_op jit(solution)/shard_map/while/body/eval_jaxpr/ppermute | solution.py:12
  116.5 9.0 %collective-permute-start.4 = (bf16[128,1024]{0,1:T(8,128)(2,1)S(1)}, bf16[128,1024]{0,1:T(8,128)(2,1)S(1)}, u32[]{:S(2)}, u32[]{:S(2)}) collective-permute-start(bf16[128,1024]{0,1:T(8,128)(2,1)S(1)} %get-tuple-element.651), channel_id=1, source_target_pairs={{4,0},{8,4},{12,8},{16,12},{20,16},{24,20},{28,24},{5,1},{9,5},{13... | collective-permute-start | bytes 786440 | tf_op jit(solution)/shard_map/while/body/eval_jaxpr/ppermute | solution.py:12
  126.5 9.3 %collective-permute-start.2 = (bf16[128,1024]{0,1:T(8,128)(2,1)S(1)}, bf16[128,1024]{0,1:T(8,128)(2,1)S(1)}, u32[]{:S(2)}, u32[]{:S(2)}) collective-permute-start(bf16[128,1024]{0,1:T(8,128)(2,1)S(1)} %get-tuple-element.650), channel_id=1, source_target_pairs={{4,0},{8,4},{12,8},{16,12},{20,16},{24,20},{28,24},{5,1},{9,5},{13... | collective-permute-start | bytes 786440 | tf_op jit(solution)/shard_map/while/body/eval_jaxpr/ppermute | solution.py:12
  127.8 8.0 %collective-permute-start.3 = (bf16[128,4,8]{0,2,1:T(8,128)(2,1)S(1)}, bf16[128,4,8]{0,2,1:T(8,128)(2,1)S(1)}, u32[]{:S(2)}, u32[]{:S(2)}) collective-permute-start(bf16[128,4,8]{0,2,1:T(8,128)(2,1)S(1)} %get-tuple-element.652), channel_id=1, source_target_pairs={{4,0},{8,4},{12,8},{16,12},{20,16},{24,20},{28,24},{5,1},{9,5},{13... | collective-permute-start | bytes 24584 | tf_op jit(solution)/shard_map/while/body/eval_jaxpr/ppermute | solution.py:12
  129.1 9.0 %collective-permute-start.4 = (bf16[128,1024]{0,1:T(8,128)(2,1)S(1)}, bf16[128,1024]{0,1:T(8,128)(2,1)S(1)}, u32[]{:S(2)}, u32[]{:S(2)}) collective-permute-start(bf16[128,1024]{0,1:T(8,128)(2,1)S(1)} %get-tuple-element.651), channel_id=1, source_target_pairs={{4,0},{8,4},{12,8},{16,12},{20,16},{24,20},{28,24},{5,1},{9,5},{13... | collective-permute-start | bytes 786440 | tf_op jit(solution)/shard_map/while/body/eval_jaxpr/ppermute | solution.py:12
  139.1 9.3 %collective-permute-start.2 = (bf16[128,1024]{0,1:T(8,128)(2,1)S(1)}, bf16[128,1024]{0,1:T(8,128)(2,1)S(1)}, u32[]{:S(2)}, u32[]{:S(2)}) collective-permute-start(bf16[128,1024]{0,1:T(8,128)(2,1)S(1)} %get-tuple-element.650), channel_id=1, source_target_pairs={{4,0},{8,4},{12,8},{16,12},{20,16},{24,20},{28,24},{5,1},{9,5},{13... | collective-permute-start | bytes 786440 | tf_op jit(solution)/shard_map/while/body/eval_jaxpr/ppermute | solution.py:12
  140.4 8.0 %collective-permute-start.3 = (bf16[128,4,8]{0,2,1:T(8,128)(2,1)S(1)}, bf16[128,4,8]{0,2,1:T(8,128)(2,1)S(1)}, u32[]{:S(2)}, u32[]{:S(2)}) collective-permute-start(bf16[128,4,8]{0,2,1:T(8,128)(2,1)S(1)} %get-tuple-element.652), channel_id=1, source_target_pairs={{4,0},{8,4},{12,8},{16,12},{20,16},{24,20},{28,24},{5,1},{9,5},{13... | collective-permute-start | bytes 24584 | tf_op jit(solution)/shard_map/while/body/eval_jaxpr/ppermute | solution.py:12
  141.7 8.9 %collective-permute-start.4 = (bf16[128,1024]{0,1:T(8,128)(2,1)S(1)}, bf16[128,1024]{0,1:T(8,128)(2,1)S(1)}, u32[]{:S(2)}, u32[]{:S(2)}) collective-permute-start(bf16[128,1024]{0,1:T(8,128)(2,1)S(1)} %get-tuple-element.651), channel_id=1, source_target_pairs={{4,0},{8,4},{12,8},{16,12},{20,16},{24,20},{28,24},{5,1},{9,5},{13... | collective-permute-start | bytes 786440 | tf_op jit(solution)/shard_map/while/body/eval_jaxpr/ppermute | solution.py:12
  151.6 9.3 %collective-permute-start.2 = (bf16[128,1024]{0,1:T(8,128)(2,1)S(1)}, bf16[128,1024]{0,1:T(8,128)(2,1)S(1)}, u32[]{:S(2)}, u32[]{:S(2)}) collective-permute-start(bf16[128,1024]{0,1:T(8,128)(2,1)S(1)} %get-tuple-element.650), channel_id=1, source_target_pairs={{4,0},{8,4},{12,8},{16,12},{20,16},{24,20},{28,24},{5,1},{9,5},{13... | collective-permute-start | bytes 786440 | tf_op jit(solution)/shard_map/while/body/eval_jaxpr/ppermute | solution.py:12
  152.9 8.0 %collective-permute-start.3 = (bf16[128,4,8]{0,2,1:T(8,128)(2,1)S(1)}, bf16[128,4,8]{0,2,1:T(8,128)(2,1)S(1)}, u32[]{:S(2)}, u32[]{:S(2)}) collective-permute-start(bf16[128,4,8]{0,2,1:T(8,128)(2,1)S(1)} %get-tuple-element.652), channel_id=1, source_target_pairs={{4,0},{8,4},{12,8},{16,12},{20,16},{24,20},{28,24},{5,1},{9,5},{13... | collective-permute-start | bytes 24584 | tf_op jit(solution)/shard_map/while/body/eval_jaxpr/ppermute | solution.py:12
  154.2 8.9 %collective-permute-start.4 = (bf16[128,1024]{0,1:T(8,128)(2,1)S(1)}, bf16[128,1024]{0,1:T(8,128)(2,1)S(1)}, u32[]{:S(2)}, u32[]{:S(2)}) collective-permute-start(bf16[128,1024]{0,1:T(8,128)(2,1)S(1)} %get-tuple-element.651), channel_id=1, source_target_pairs={{4,0},{8,4},{12,8},{16,12},{20,16},{24,20},{28,24},{5,1},{9,5},{13... | collective-permute-start | bytes 786440 | tf_op jit(solution)/shard_map/while/body/eval_jaxpr/ppermute | solution.py:12
  164.2 9.3 %collective-permute-start.2 = (bf16[128,1024]{0,1:T(8,128)(2,1)S(1)}, bf16[128,1024]{0,1:T(8,128)(2,1)S(1)}, u32[]{:S(2)}, u32[]{:S(2)}) collective-permute-start(bf16[128,1024]{0,1:T(8,128)(2,1)S(1)} %get-tuple-element.650), channel_id=1, source_target_pairs={{4,0},{8,4},{12,8},{16,12},{20,16},{24,20},{28,24},{5,1},{9,5},{13... | collective-permute-start | bytes 786440 | tf_op jit(solution)/shard_map/while/body/eval_jaxpr/ppermute | solution.py:12
  166.8 8.9 %collective-permute-start.4 = (bf16[128,1024]{0,1:T(8,128)(2,1)S(1)}, bf16[128,1024]{0,1:T(8,128)(2,1)S(1)}, u32[]{:S(2)}, u32[]{:S(2)}) collective-permute-start(bf16[128,1024]{0,1:T(8,128)(2,1)S(1)} %get-tuple-element.651), channel_id=1, source_target_pairs={{4,0},{8,4},{12,8},{16,12},{20,16},{24,20},{28,24},{5,1},{9,5},{13... | collective-permute-start | bytes 786440 | tf_op jit(solution)/shard_map/while/body/eval_jaxpr/ppermute | solution.py:12
  (24 other events, 117.9 us)
where the time goes:
time: 254 us; the launch traced here: 253 us
  starting transfers between devices  92.3 us (36%)
  waiting for transfers between devices  54.4 us (21%)
  blocking collectives  44.9 us (18%)
  matrix products  43.7 us (17%)
  other arithmetic  8.44 us (3%)
  local copies, waits for them, and re-layouts  6.71 us (3%)
    ppermute x36, starting transfers between devices, from_behind(): lax.ppermute(value, axis, [(source, source + steps) for source in range(l...  92.3 us
    ppermute x36, waiting for transfers between devices, from_behind(): lax.ppermute(value, axis, [(source, source + steps) for source in range(l...  54.4 us
    psum x1, blocking collectives, local(): filter_total = lax.psum(local_terms, ('seq', 'tp'))  44.9 us
    conv_general_dilated x1, matrix products, local(): lax.conv_general_dilated(padded[None], mixed[:, None, :], (1,), 'VALID',...  11.7 us
    conv_general_dilated x1, matrix products, local(): lax.conv_general_dilated(padded[None], taps[:, None, :], (1,), 'VALID', d...  11.6 us
    dot_general x8, matrix products, query_tile(): jnp.einsum('hqk,khd->qhd', weights * (dprob - delta_heads[:, :, None]), k...  5.68 us
  transfers between devices with their start and end apart: 36, of which 21 were waited for; matrix products, arithmetic and copies ran while one was open for 11% of the time, Pallas kernels for 0%

commit v1 on v0

--- a/solution.py
+++ b/solution.py
@@ -174,7 +174,7 @@
     grad_feat_k = (dw * feat_v.astype(jnp.float32)).astype(jnp.bfloat16)
     grad_feat_v = (dw * feat_k.astype(jnp.float32)).astype(jnp.bfloat16)
     local_terms = jnp.sum(local_terms.reshape(span_taps, channels // groups, groups), axis=1).T
-    filter_total = lax.psum(local_terms, ("seq", "tp"))
+    filter_total = jnp.sum(lax.all_gather(local_terms, ("seq", "tp")), axis=0)
     count_all = rows * shards * channels * lax.axis_size("tp") / groups
     grad_filters = filter_total * (1.0 / count_all**0.5)
     return (grad_q, grad_k, grad_v, grad_gate, grad_feat_k, grad_feat_v, grad_filters)

time: 254 us -> 239 us (0.941)
  the two profiles are of different devices: /device:TPU:0 before, /device:TPU:23 now
where the time goes in v1:
time: 239 us; the launch traced here: 238 us
  starting transfers between devices  89.9 us (38%)
  waiting for transfers between devices  63.5 us (27%)
  matrix products  44.1 us (18%)
  local copies, waits for them, and re-layouts  14.4 us (6%)
  between operations  14.4 us (6%)
  other arithmetic  10.4 us (4%)
    ppermute x36, starting transfers between devices, from_behind(): lax.ppermute(value, axis, [(source, source + steps) for source in range(l...  89.9 us
    ppermute x36, waiting for transfers between devices, from_behind(): lax.ppermute(value, axis, [(source, source + steps) for source in range(l...  63.5 us
    conv_general_dilated x1, matrix products, local(): lax.conv_general_dilated(padded[None], mixed[:, None, :], (1,), 'VALID',...  12.2 us
    conv_general_dilated x1, matrix products, local(): lax.conv_general_dilated(padded[None], taps[:, None, :], (1,), 'VALID', d...  11.4 us
    dot_general x8, matrix products, query_tile(): jnp.einsum('hqk,khd->qhd', weights * (dprob - delta_heads[:, :, None]), k...  5.68 us
    while x42, local copies, waits for them, and re-layouts  5.36 us
  transfers between devices with their start and end apart: 37, of which 28 were waited for; matrix products, arithmetic and copies ran while one was open for 14% of the time, Pallas kernels for 0%

profile of v1, /device:TPU:23, one launch (start us, length us, event | category | flops | bytes accessed | tf_op | source)
XLA Modules:
  0.0 237.8 jit_solution(14766460130722222464)
XLA Ops:
  7.2 2.7 %fusion.19 = (bf16[128,2048]{1,0:T(8,128)(2,1)}, bf16[128,2048]{1,0:T(8,128)(2,1)}) fusion(bf16[128,2048]{1,0:T(8,128)(2,1)} %param.24, bf16[128,2048]{1,0:T(8,128)(2,1)} %param.20, bf16[128,2048]{1,0:T(8,128)(2,1)} %param.23), kind=kLoop, calls=%fused_computation.41 | loop fusion | flops 1835008 | bytes 2621440 | tf_op jit(solution)/shard_map/convert_element_type | solution.py:149
  9.9 2.7 %collective-permute-start.5 = (bf16[127,2048]{1,0:T(8,128)(2,1)}, bf16[127,2048]{1,0:T(8,128)(2,1)}, u32[]{:S(2)}, u32[]{:S(2)}) collective-permute-start(bf16[127,2048]{1,0:T(8,128)(2,1)} %bitcast.111), channel_id=1, source_target_pairs={{4,0},{8,4},{12,8},{16,12},{20,16},{24,20},{28,24},{5,1},{9,5},{13... | collective-permute-start | bytes 1560584 | tf_op jit(solution)/shard_map/ppermute | solution.py:12
  16.5 80.5 %while.42 = (s32[]{:T(128)}, f32[8,128]{1,0:T(8,128)S(1)}, f32[8,128]{1,0:T(8,128)S(1)}, f32[128,8,128]{2,0,1:T(8,128)S(1)}, bf16[128,1024]{0,1:T(8,128)(2,1)S(1...) while((s32[]{:T(128)}, f32[8,128]{1,0:T(8,128)S(1)}, ...), condition=%wide.region_6.7_spmd, body=%wide.region_3.6_spmd.sunk | while | flops 270011392 | bytes 8196297 | solution.py:92
  16.5 3.1 %collective-permute-start = (bf16[128,1024]{0,1:T(8,128)(2,1)S(1)}, bf16[128,1024]{0,1:T(8,128)(2,1)S(1)}, u32[]{:S(2)}, u32[]{:S(2)}) collective-permute-start(bf16[128,1024]{0,1:T(8,128)(2,1)S(1)} %get-tuple-element.618), channel_id=1, source_target_pairs={{0,4},{4,8},{8,12},{12,16},{16,20},{20,24},{24,28},{1,5},{5,9},{9,... | collective-permute-start | bytes 786440 | tf_op jit(solution)/shard_map/while/body/eval_jaxpr/ppermute | solution.py:12
  19.7 3.2 %collective-permute-start.1 = (bf16[128,1024]{0,1:T(8,128)(2,1)S(1)}, bf16[128,1024]{0,1:T(8,128)(2,1)S(1)}, u32[]{:S(2)}, u32[]{:S(2)}) collective-permute-start(bf16[128,1024]{0,1:T(8,128)(2,1)S(1)} %get-tuple-element.619), channel_id=1, source_target_pairs={{0,4},{4,8},{8,12},{12,16},{16,20},{20,24},{24,28},{1,5},{5,9},{9,... | collective-permute-start | bytes 786440 | tf_op jit(solution)/shard_map/while/body/eval_jaxpr/ppermute | solution.py:12
  23.4 2.7 %collective-permute-done.1 = bf16[128,1024]{0,1:T(8,128)(2,1)S(1)} collective-permute-done((bf16[128,1024]{0,1:T(8,128)(2,1)S(1)}, bf16[128,1024]{0,1:T(8,128)(2,1)S(1)}, u32[]{:S(2)}, u32[]{:S(2)}) %collective-permute-start.1) | collective-permute-done | bytes 262176 | tf_op jit(solution)/shard_map/while/body/eval_jaxpr/ppermute | solution.py:12
  27.3 4.4 %collective-permute-start = (bf16[128,1024]{0,1:T(8,128)(2,1)S(1)}, bf16[128,1024]{0,1:T(8,128)(2,1)S(1)}, u32[]{:S(2)}, u32[]{:S(2)}) collective-permute-start(bf16[128,1024]{0,1:T(8,128)(2,1)S(1)} %get-tuple-element.618), channel_id=1, source_target_pairs={{0,4},{4,8},{8,12},{12,16},{16,20},{20,24},{24,28},{1,5},{5,9},{9,... | collective-permute-start | bytes 786440 | tf_op jit(solution)/shard_map/while/body/eval_jaxpr/ppermute | solution.py:12
  38.9 4.4 %collective-permute-start = (bf16[128,1024]{0,1:T(8,128)(2,1)S(1)}, bf16[128,1024]{0,1:T(8,128)(2,1)S(1)}, u32[]{:S(2)}, u32[]{:S(2)}) collective-permute-start(bf16[128,1024]{0,1:T(8,128)(2,1)S(1)} %get-tuple-element.618), channel_id=1, source_target_pairs={{0,4},{4,8},{8,12},{12,16},{16,20},{20,24},{24,28},{1,5},{5,9},{9,... | collective-permute-start | bytes 786440 | tf_op jit(solution)/shard_map/while/body/eval_jaxpr/ppermute | solution.py:12
  50.6 4.4 %collective-permute-start = (bf16[128,1024]{0,1:T(8,128)(2,1)S(1)}, bf16[128,1024]{0,1:T(8,128)(2,1)S(1)}, u32[]{:S(2)}, u32[]{:S(2)}) collective-permute-start(bf16[128,1024]{0,1:T(8,128)(2,1)S(1)} %get-tuple-element.618), channel_id=1, source_target_pairs={{0,4},{4,8},{8,12},{12,16},{16,20},{20,24},{24,28},{1,5},{5,9},{9,... | collective-permute-start | bytes 786440 | tf_op jit(solution)/shard_map/while/body/eval_jaxpr/ppermute | solution.py:12
  62.2 4.4 %collective-permute-start = (bf16[128,1024]{0,1:T(8,128)(2,1)S(1)}, bf16[128,1024]{0,1:T(8,128)(2,1)S(1)}, u32[]{:S(2)}, u32[]{:S(2)}) collective-permute-start(bf16[128,1024]{0,1:T(8,128)(2,1)S(1)} %get-tuple-element.618), channel_id=1, source_target_pairs={{0,4},{4,8},{8,12},{12,16},{16,20},{20,24},{24,28},{1,5},{5,9},{9,... | collective-permute-start | bytes 786440 | tf_op jit(solution)/shard_map/while/body/eval_jaxpr/ppermute | solution.py:12
  73.8 4.4 %collective-permute-start = (bf16[128,1024]{0,1:T(8,128)(2,1)S(1)}, bf16[128,1024]{0,1:T(8,128)(2,1)S(1)}, u32[]{:S(2)}, u32[]{:S(2)}) collective-permute-start(bf16[128,1024]{0,1:T(8,128)(2,1)S(1)} %get-tuple-element.618), channel_id=1, source_target_pairs={{0,4},{4,8},{8,12},{12,16},{16,20},{20,24},{24,28},{1,5},{5,9},{9,... | collective-permute-start | bytes 786440 | tf_op jit(solution)/shard_map/while/body/eval_jaxpr/ppermute | solution.py:12
  85.4 4.4 %collective-permute-start = (bf16[128,1024]{0,1:T(8,128)(2,1)S(1)}, bf16[128,1024]{0,1:T(8,128)(2,1)S(1)}, u32[]{:S(2)}, u32[]{:S(2)}) collective-permute-start(bf16[128,1024]{0,1:T(8,128)(2,1)S(1)} %get-tuple-element.618), channel_id=1, source_target_pairs={{0,4},{4,8},{8,12},{12,16},{16,20},{20,24},{24,28},{1,5},{5,9},{9,... | collective-permute-start | bytes 786440 | tf_op jit(solution)/shard_map/while/body/eval_jaxpr/ppermute | solution.py:12
  102.1 11.4 %fusion.15 = f32[1,128,2048]{2,0,1:T(1,128)S(1)} fusion(f32[128,1,2048]{2,1,0:T(1,128)S(1)} %copy-done.4, bf16[1,255,2048]{2,1,0:T(8,128)(2,1)S(1)} %maximum_bitcast_fusion), kind=kOutput, calls=%fused_computation.28 | convolution fusion | flops 402653184 | bytes 3141632 | tf_op jit(solution)/shard_map/conv_general_dilated | solution.py:156
  115.1 12.2 %fusion.13 = f32[1,128,2048]{2,0,1:T(1,128)} fusion(bf16[1,255,2048]{2,1,0:T(8,128)(2,1)S(1)} %maximum_bitcast_fusion, f32[128,1,2048]{2,0,1:T(8,128)S(1)} %get-tuple-element.462), kind=kOutput, calls=%fused_computation.26 | convolution fusion | flops 402653184 | bytes 3141632 | tf_op jit(solution)/shard_map/conv_general_dilated | solution.py:165
  130.4 96.1 %while.43 = (s32[]{:T(128)}, f32[128,8,128]{2,0,1:T(8,128)S(1)}, f32[128,8,128]{2,0,1:T(8,128)S(1)}, bf16[128,1024]{0,1:T(8,128)(2,1)}, bf16[128,1024]{0,1:T(8,1...) while((s32[]{:T(128)}, f32[128,8,128]{2,0,1:T(8,128)S(1)}, ...), condition=%wide.region_8.9_spmd, body=%wide.region_7.8_spmd.sunk | while | flops 135403520 | bytes 8462587 | solution.py:141
  130.4 2.8 %collective-permute-start.2 = (bf16[128,1024]{0,1:T(8,128)(2,1)}, bf16[128,1024]{0,1:T(8,128)(2,1)S(1)}, u32[]{:S(2)}, u32[]{:S(2)}) collective-permute-start(bf16[128,1024]{0,1:T(8,128)(2,1)} %get-tuple-element.650), channel_id=1, source_target_pairs={{4,0},{8,4},{12,8},{16,12},{20,16},{24,20},{28,24},{5,1},{9,5},{13... | collective-permute-start | bytes 786440 | tf_op jit(solution)/shard_map/while/body/eval_jaxpr/ppermute | solution.py:12
  139.5 3.7 %collective-permute-done.4 = bf16[128,1024]{0,1:T(8,128)(2,1)S(1)} collective-permute-done((bf16[128,1024]{0,1:T(8,128)(2,1)S(1)}, bf16[128,1024]{0,1:T(8,128)(2,1)S(1)}, u32[]{:S(2)}, u32[]{:S(2)}) %collective-permute-start.4) | collective-permute-done | bytes 262176 | tf_op jit(solution)/shard_map/while/body/eval_jaxpr/ppermute | solution.py:12
  153.3 3.3 %collective-permute-done.4 = bf16[128,1024]{0,1:T(8,128)(2,1)S(1)} collective-permute-done((bf16[128,1024]{0,1:T(8,128)(2,1)S(1)}, bf16[128,1024]{0,1:T(8,128)(2,1)S(1)}, u32[]{:S(2)}, u32[]{:S(2)}) %collective-permute-start.4) | collective-permute-done | bytes 262176 | tf_op jit(solution)/shard_map/while/body/eval_jaxpr/ppermute | solution.py:12
  164.0 3.0 %collective-permute-done.3 = bf16[128,4,8]{0,2,1:T(8,128)(2,1)S(1)} collective-permute-done((bf16[128,4,8]{0,2,1:T(8,128)(2,1)S(1)}, bf16[128,4,8]{0,2,1:T(8,128)(2,1)S(1)}, u32[]{:S(2)}, u32[]{:S(2)}) %collective-permute-start.3) | collective-permute-done | bytes 8224 | tf_op jit(solution)/shard_map/while/body/eval_jaxpr/ppermute | solution.py:12
  177.4 3.5 %collective-permute-done.3 = bf16[128,4,8]{0,2,1:T(8,128)(2,1)S(1)} collective-permute-done((bf16[128,4,8]{0,2,1:T(8,128)(2,1)S(1)}, bf16[128,4,8]{0,2,1:T(8,128)(2,1)S(1)}, u32[]{:S(2)}, u32[]{:S(2)}) %collective-permute-start.3) | collective-permute-done | bytes 8224 | tf_op jit(solution)/shard_map/while/body/eval_jaxpr/ppermute | solution.py:12
  181.2 2.9 %collective-permute-done.4 = bf16[128,1024]{0,1:T(8,128)(2,1)S(1)} collective-permute-done((bf16[128,1024]{0,1:T(8,128)(2,1)S(1)}, bf16[128,1024]{0,1:T(8,128)(2,1)S(1)}, u32[]{:S(2)}, u32[]{:S(2)}) %collective-permute-start.4) | collective-permute-done | bytes 262176 | tf_op jit(solution)/shard_map/while/body/eval_jaxpr/ppermute | solution.py:12
  194.1 3.7 %collective-permute-done.4 = bf16[128,1024]{0,1:T(8,128)(2,1)S(1)} collective-permute-done((bf16[128,1024]{0,1:T(8,128)(2,1)S(1)}, bf16[128,1024]{0,1:T(8,128)(2,1)S(1)}, u32[]{:S(2)}, u32[]{:S(2)}) %collective-permute-start.4) | collective-permute-done | bytes 262176 | tf_op jit(solution)/shard_map/while/body/eval_jaxpr/ppermute | solution.py:12
  207.8 3.7 %collective-permute-done.4 = bf16[128,1024]{0,1:T(8,128)(2,1)S(1)} collective-permute-done((bf16[128,1024]{0,1:T(8,128)(2,1)S(1)}, bf16[128,1024]{0,1:T(8,128)(2,1)S(1)}, u32[]{:S(2)}, u32[]{:S(2)}) %collective-permute-start.4) | collective-permute-done | bytes 262176 | tf_op jit(solution)/shard_map/while/body/eval_jaxpr/ppermute | solution.py:12
  221.6 3.2 %collective-permute-done.4 = bf16[128,1024]{0,1:T(8,128)(2,1)S(1)} collective-permute-done((bf16[128,1024]{0,1:T(8,128)(2,1)S(1)}, bf16[128,1024]{0,1:T(8,128)(2,1)S(1)}, u32[]{:S(2)}, u32[]{:S(2)}) %collective-permute-start.4) | collective-permute-done | bytes 262176 | tf_op jit(solution)/shard_map/while/body/eval_jaxpr/ppermute | solution.py:12
  (235 shorter events, 128.2 us)
Async XLA Ops:
  7.2 221.9 %all-gather.3.cloned.1.call-start = ((), (), s32[]{:S(2)}) async-start(), calls=%async_computation | async-start | bytes 1081344 | tf_op jit(solution)/shard_map/all_gather | solution.py:177
  9.9 90.7 %collective-permute-start.5 = (bf16[127,2048]{1,0:T(8,128)(2,1)}, bf16[127,2048]{1,0:T(8,128)(2,1)}, u32[]{:S(2)}, u32[]{:S(2)}) collective-permute-start(bf16[127,2048]{1,0:T(8,128)(2,1)} %bitcast.111), channel_id=1, source_target_pairs={{4,0},{8,4},{12,8},{16,12},{20,16},{24,20},{28,24},{5,1},{9,5},{13... | collective-permute-start | bytes 1560584 | tf_op jit(solution)/shard_map/ppermute | solution.py:12
  27.3 7.7 %collective-permute-start = (bf16[128,1024]{0,1:T(8,128)(2,1)S(1)}, bf16[128,1024]{0,1:T(8,128)(2,1)S(1)}, u32[]{:S(2)}, u32[]{:S(2)}) collective-permute-start(bf16[128,1024]{0,1:T(8,128)(2,1)S(1)} %get-tuple-element.618), channel_id=1, source_target_pairs={{0,4},{4,8},{8,12},{12,16},{16,20},{20,24},{24,28},{1,5},{5,9},{9,... | collective-permute-start | bytes 786440 | tf_op jit(solution)/shard_map/while/body/eval_jaxpr/ppermute | solution.py:12
  38.9 7.7 %collective-permute-start = (bf16[128,1024]{0,1:T(8,128)(2,1)S(1)}, bf16[128,1024]{0,1:T(8,128)(2,1)S(1)}, u32[]{:S(2)}, u32[]{:S(2)}) collective-permute-start(bf16[128,1024]{0,1:T(8,128)(2,1)S(1)} %get-tuple-element.618), channel_id=1, source_target_pairs={{0,4},{4,8},{8,12},{12,16},{16,20},{20,24},{24,28},{1,5},{5,9},{9,... | collective-permute-start | bytes 786440 | tf_op jit(solution)/shard_map/while/body/eval_jaxpr/ppermute | solution.py:12
  50.6 7.7 %collective-permute-start = (bf16[128,1024]{0,1:T(8,128)(2,1)S(1)}, bf16[128,1024]{0,1:T(8,128)(2,1)S(1)}, u32[]{:S(2)}, u32[]{:S(2)}) collective-permute-start(bf16[128,1024]{0,1:T(8,128)(2,1)S(1)} %get-tuple-element.618), channel_id=1, source_target_pairs={{0,4},{4,8},{8,12},{12,16},{16,20},{20,24},{24,28},{1,5},{5,9},{9,... | collective-permute-start | bytes 786440 | tf_op jit(solution)/shard_map/while/body/eval_jaxpr/ppermute | solution.py:12
  62.2 7.7 %collective-permute-start = (bf16[128,1024]{0,1:T(8,128)(2,1)S(1)}, bf16[128,1024]{0,1:T(8,128)(2,1)S(1)}, u32[]{:S(2)}, u32[]{:S(2)}) collective-permute-start(bf16[128,1024]{0,1:T(8,128)(2,1)S(1)} %get-tuple-element.618), channel_id=1, source_target_pairs={{0,4},{4,8},{8,12},{12,16},{16,20},{20,24},{24,28},{1,5},{5,9},{9,... | collective-permute-start | bytes 786440 | tf_op jit(solution)/shard_map/while/body/eval_jaxpr/ppermute | solution.py:12
  73.8 7.7 %collective-permute-start = (bf16[128,1024]{0,1:T(8,128)(2,1)S(1)}, bf16[128,1024]{0,1:T(8,128)(2,1)S(1)}, u32[]{:S(2)}, u32[]{:S(2)}) collective-permute-start(bf16[128,1024]{0,1:T(8,128)(2,1)S(1)} %get-tuple-element.618), channel_id=1, source_target_pairs={{0,4},{4,8},{8,12},{12,16},{16,20},{20,24},{24,28},{1,5},{5,9},{9,... | collective-permute-start | bytes 786440 | tf_op jit(solution)/shard_map/while/body/eval_jaxpr/ppermute | solution.py:12
  85.4 7.7 %collective-permute-start = (bf16[128,1024]{0,1:T(8,128)(2,1)S(1)}, bf16[128,1024]{0,1:T(8,128)(2,1)S(1)}, u32[]{:S(2)}, u32[]{:S(2)}) collective-permute-start(bf16[128,1024]{0,1:T(8,128)(2,1)S(1)} %get-tuple-element.618), channel_id=1, source_target_pairs={{0,4},{4,8},{8,12},{12,16},{16,20},{20,24},{24,28},{1,5},{5,9},{9,... | collective-permute-start | bytes 786440 | tf_op jit(solution)/shard_map/while/body/eval_jaxpr/ppermute | solution.py:12
  130.4 8.7 %collective-permute-start.2 = (bf16[128,1024]{0,1:T(8,128)(2,1)}, bf16[128,1024]{0,1:T(8,128)(2,1)S(1)}, u32[]{:S(2)}, u32[]{:S(2)}) collective-permute-start(bf16[128,1024]{0,1:T(8,128)(2,1)} %get-tuple-element.650), channel_id=1, source_target_pairs={{4,0},{8,4},{12,8},{16,12},{20,16},{24,20},{28,24},{5,1},{9,5},{13... | collective-permute-start | bytes 786440 | tf_op jit(solution)/shard_map/while/body/eval_jaxpr/ppermute | solution.py:12
  135.1 8.1 %collective-permute-start.4 = (bf16[128,1024]{0,1:T(8,128)(2,1)S(1)}, bf16[128,1024]{0,1:T(8,128)(2,1)S(1)}, u32[]{:S(2)}, u32[]{:S(2)}) collective-permute-start(bf16[128,1024]{0,1:T(8,128)(2,1)S(1)} %get-tuple-element.651), channel_id=1, source_target_pairs={{4,0},{8,4},{12,8},{16,12},{20,16},{24,20},{28,24},{5,1},{9,5},{13... | collective-permute-start | bytes 786440 | tf_op jit(solution)/shard_map/while/body/eval_jaxpr/ppermute | solution.py:12
  144.9 8.1 %collective-permute-start.2 = (bf16[128,1024]{0,1:T(8,128)(2,1)}, bf16[128,1024]{0,1:T(8,128)(2,1)S(1)}, u32[]{:S(2)}, u32[]{:S(2)}) collective-permute-start(bf16[128,1024]{0,1:T(8,128)(2,1)} %get-tuple-element.650), channel_id=1, source_target_pairs={{4,0},{8,4},{12,8},{16,12},{20,16},{24,20},{28,24},{5,1},{9,5},{13... | collective-permute-start | bytes 786440 | tf_op jit(solution)/shard_map/while/body/eval_jaxpr/ppermute | solution.py:12
  148.9 7.7 %collective-permute-start.4 = (bf16[128,1024]{0,1:T(8,128)(2,1)S(1)}, bf16[128,1024]{0,1:T(8,128)(2,1)S(1)}, u32[]{:S(2)}, u32[]{:S(2)}) collective-permute-start(bf16[128,1024]{0,1:T(8,128)(2,1)S(1)} %get-tuple-element.651), channel_id=1, source_target_pairs={{4,0},{8,4},{12,8},{16,12},{20,16},{24,20},{28,24},{5,1},{9,5},{13... | collective-permute-start | bytes 786440 | tf_op jit(solution)/shard_map/while/body/eval_jaxpr/ppermute | solution.py:12
  158.2 8.8 %collective-permute-start.2 = (bf16[128,1024]{0,1:T(8,128)(2,1)}, bf16[128,1024]{0,1:T(8,128)(2,1)S(1)}, u32[]{:S(2)}, u32[]{:S(2)}) collective-permute-start(bf16[128,1024]{0,1:T(8,128)(2,1)} %get-tuple-element.650), channel_id=1, source_target_pairs={{4,0},{8,4},{12,8},{16,12},{20,16},{24,20},{28,24},{5,1},{9,5},{13... | collective-permute-start | bytes 786440 | tf_op jit(solution)/shard_map/while/body/eval_jaxpr/ppermute | solution.py:12
  160.1 6.9 %collective-permute-start.3 = (bf16[128,4,8]{0,2,1:T(8,128)(2,1)S(1)}, bf16[128,4,8]{0,2,1:T(8,128)(2,1)S(1)}, u32[]{:S(2)}, u32[]{:S(2)}) collective-permute-start(bf16[128,4,8]{0,2,1:T(8,128)(2,1)S(1)} %get-tuple-element.652), channel_id=1, source_target_pairs={{4,0},{8,4},{12,8},{16,12},{20,16},{24,20},{28,24},{5,1},{9,5},{13... | collective-permute-start | bytes 24584 | tf_op jit(solution)/shard_map/while/body/eval_jaxpr/ppermute | solution.py:12
  162.1 7.7 %collective-permute-start.4 = (bf16[128,1024]{0,1:T(8,128)(2,1)S(1)}, bf16[128,1024]{0,1:T(8,128)(2,1)S(1)}, u32[]{:S(2)}, u32[]{:S(2)}) collective-permute-start(bf16[128,1024]{0,1:T(8,128)(2,1)S(1)} %get-tuple-element.651), channel_id=1, source_target_pairs={{4,0},{8,4},{12,8},{16,12},{20,16},{24,20},{28,24},{5,1},{9,5},{13... | collective-permute-start | bytes 786440 | tf_op jit(solution)/shard_map/while/body/eval_jaxpr/ppermute | solution.py:12
  171.4 9.4 %collective-permute-start.2 = (bf16[128,1024]{0,1:T(8,128)(2,1)}, bf16[128,1024]{0,1:T(8,128)(2,1)S(1)}, u32[]{:S(2)}, u32[]{:S(2)}) collective-permute-start(bf16[128,1024]{0,1:T(8,128)(2,1)} %get-tuple-element.650), channel_id=1, source_target_pairs={{4,0},{8,4},{12,8},{16,12},{20,16},{24,20},{28,24},{5,1},{9,5},{13... | collective-permute-start | bytes 786440 | tf_op jit(solution)/shard_map/while/body/eval_jaxpr/ppermute | solution.py:12
  173.4 7.5 %collective-permute-start.3 = (bf16[128,4,8]{0,2,1:T(8,128)(2,1)S(1)}, bf16[128,4,8]{0,2,1:T(8,128)(2,1)S(1)}, u32[]{:S(2)}, u32[]{:S(2)}) collective-permute-start(bf16[128,4,8]{0,2,1:T(8,128)(2,1)S(1)} %get-tuple-element.652), channel_id=1, source_target_pairs={{4,0},{8,4},{12,8},{16,12},{20,16},{24,20},{28,24},{5,1},{9,5},{13... | collective-permute-start | bytes 24584 | tf_op jit(solution)/shard_map/while/body/eval_jaxpr/ppermute | solution.py:12
  175.4 8.6 %collective-permute-start.4 = (bf16[128,1024]{0,1:T(8,128)(2,1)S(1)}, bf16[128,1024]{0,1:T(8,128)(2,1)S(1)}, u32[]{:S(2)}, u32[]{:S(2)}) collective-permute-start(bf16[128,1024]{0,1:T(8,128)(2,1)S(1)} %get-tuple-element.651), channel_id=1, source_target_pairs={{4,0},{8,4},{12,8},{16,12},{20,16},{24,20},{28,24},{5,1},{9,5},{13... | collective-permute-start | bytes 786440 | tf_op jit(solution)/shard_map/while/body/eval_jaxpr/ppermute | solution.py:12
  185.7 8.0 %collective-permute-start.2 = (bf16[128,1024]{0,1:T(8,128)(2,1)}, bf16[128,1024]{0,1:T(8,128)(2,1)S(1)}, u32[]{:S(2)}, u32[]{:S(2)}) collective-permute-start(bf16[128,1024]{0,1:T(8,128)(2,1)} %get-tuple-element.650), channel_id=1, source_target_pairs={{4,0},{8,4},{12,8},{16,12},{20,16},{24,20},{28,24},{5,1},{9,5},{13... | collective-permute-start | bytes 786440 | tf_op jit(solution)/shard_map/while/body/eval_jaxpr/ppermute | solution.py:12
  190.1 7.7 %collective-permute-start.4 = (bf16[128,1024]{0,1:T(8,128)(2,1)S(1)}, bf16[128,1024]{0,1:T(8,128)(2,1)S(1)}, u32[]{:S(2)}, u32[]{:S(2)}) collective-permute-start(bf16[128,1024]{0,1:T(8,128)(2,1)S(1)} %get-tuple-element.651), channel_id=1, source_target_pairs={{4,0},{8,4},{12,8},{16,12},{20,16},{24,20},{28,24},{5,1},{9,5},{13... | collective-permute-start | bytes 786440 | tf_op jit(solution)/shard_map/while/body/eval_jaxpr/ppermute | solution.py:12
  199.5 8.0 %collective-permute-start.2 = (bf16[128,1024]{0,1:T(8,128)(2,1)}, bf16[128,1024]{0,1:T(8,128)(2,1)S(1)}, u32[]{:S(2)}, u32[]{:S(2)}) collective-permute-start(bf16[128,1024]{0,1:T(8,128)(2,1)} %get-tuple-element.650), channel_id=1, source_target_pairs={{4,0},{8,4},{12,8},{16,12},{20,16},{24,20},{28,24},{5,1},{9,5},{13... | collective-permute-start | bytes 786440 | tf_op jit(solution)/shard_map/while/body/eval_jaxpr/ppermute | solution.py:12
  203.9 7.7 %collective-permute-start.4 = (bf16[128,1024]{0,1:T(8,128)(2,1)S(1)}, bf16[128,1024]{0,1:T(8,128)(2,1)S(1)}, u32[]{:S(2)}, u32[]{:S(2)}) collective-permute-start(bf16[128,1024]{0,1:T(8,128)(2,1)S(1)} %get-tuple-element.651), channel_id=1, source_target_pairs={{4,0},{8,4},{12,8},{16,12},{20,16},{24,20},{28,24},{5,1},{9,5},{13... | collective-permute-start | bytes 786440 | tf_op jit(solution)/shard_map/while/body/eval_jaxpr/ppermute | solution.py:12
  213.3 8.0 %collective-permute-start.2 = (bf16[128,1024]{0,1:T(8,128)(2,1)}, bf16[128,1024]{0,1:T(8,128)(2,1)S(1)}, u32[]{:S(2)}, u32[]{:S(2)}) collective-permute-start(bf16[128,1024]{0,1:T(8,128)(2,1)} %get-tuple-element.650), channel_id=1, source_target_pairs={{4,0},{8,4},{12,8},{16,12},{20,16},{24,20},{28,24},{5,1},{9,5},{13... | collective-permute-start | bytes 786440 | tf_op jit(solution)/shard_map/while/body/eval_jaxpr/ppermute | solution.py:12
  217.1 7.7 %collective-permute-start.4 = (bf16[128,1024]{0,1:T(8,128)(2,1)S(1)}, bf16[128,1024]{0,1:T(8,128)(2,1)S(1)}, u32[]{:S(2)}, u32[]{:S(2)}) collective-permute-start(bf16[128,1024]{0,1:T(8,128)(2,1)S(1)} %get-tuple-element.651), channel_id=1, source_target_pairs={{4,0},{8,4},{12,8},{16,12},{20,16},{24,20},{28,24},{5,1},{9,5},{13... | collective-permute-start | bytes 786440 | tf_op jit(solution)/shard_map/while/body/eval_jaxpr/ppermute | solution.py:12
  (26 other events, 206.3 us)
Sparse Core Ops, SparseCore 0:
  130.5 54.3 all-gather.2
